TPU v7x, 32 devices: a whole 2x2x4 slice. The times are simulated.
32 devices in a mesh: tm: 8 (over z, x), exp: 4 (over y, core).
Axes of the slice: x: 2, y: 2, z: 4, core: 2. Of those that a mesh axis runs over, the one named last changes fastest.
Arguments:
- transitions: float32 [512, 256, 256], P('tm'), may hold values from -0.2 to 1.2
- pattern: int32 [512, 4, 4], P('tm'), may hold values from 0 to 1, as said below
- obs_mask: int32 [4, 512, 256], P('exp', 'tm'), may hold values 0 or 1
- measured: float32 [4, 512, 256], P('exp', 'tm'), may hold values from -6 to 6
- prior_mean: float32 [4, 256], P('exp'), may hold values from -6 to 6
- filter_gain: float32 [256], replicated, may hold values from 0 to 0.6
- smooth_gain: float32 [256], replicated, may hold values from 0.3 to 1
Outputs:
- smoothed: float32 [4, 512, 256], P('exp', 'tm')
- information: float32 [256, 256], replicated
Inputs may be any that keep to these rules, and one draw needn't show every extreme that they name: `pattern`: diagonal blocks are always present.
All inputs are finite; a program needn't handle non-finite values. No bound on the sum of `obs_mask` on one device may be relied on, other than what follows from the above.
Results may differ from a plain program's by a relative error of at most 0.0001.
Values sent between devices are 32-bit elements; how exact they have to be, the bound alone decides.
A program may use at most 192 MiB of HBM per device.

v0:
```python
import jax
import jax.numpy as jnp
from jax import lax
from jax.sharding import PartitionSpec as P


def entering(x, axis, combine, identity, reverse):
    length, index = (lax.axis_size(axis), lax.axis_index(axis))
    everything = jax.tree.map(lambda part: lax.all_gather(part, axis), x)
    start = jax.tree.map(
        lambda part, zero: jnp.broadcast_to(jnp.asarray(zero, part.dtype), part.shape), x, identity
    )

    def hop(k, before):
        at = length - 1 - k if reverse else k
        reached = at > index if reverse else at < index
        new = combine(before, jax.tree.map(lambda part: part[at], everything))
        return jax.tree.map(lambda a, b: jnp.where(reached, a, b), new, before)

    return lax.fori_loop(0, length, hop, start)


def masked_dense(transitions, pattern):
    count_steps, state_width, _ = transitions.shape
    block_count = pattern.shape[1]
    block_size = state_width // block_count
    reshaped = transitions.reshape(count_steps, block_count, block_size, block_count, block_size)
    weights = pattern.astype(jnp.float32)[:, :, None, :, None]
    return (reshaped * weights).reshape(count_steps, state_width, state_width)


def chain_product(matrices):
    while matrices.shape[0] > 1:
        paired = matrices.shape[0] // 2 * 2
        earlier_maps = matrices[0:paired:2]
        later_maps = matrices[1:paired:2]
        joined = jnp.einsum(
            "bij,bjk->bik", later_maps, earlier_maps, precision=lax.Precision.HIGHEST
        )
        matrices = joined
    return matrices[0]


def compose(earlier_maps, later_maps):
    highest = lax.Precision.HIGHEST
    return (
        jnp.dot(later_maps[0], earlier_maps[0], precision=highest),
        jnp.dot(later_maps[0], earlier_maps[1], precision=highest) + later_maps[1],
    )


def run_filter(dense_steps, keep_rows, drive_terms, start_state):

    def update(state, inputs):
        trans_step, keep_step, drive_step = inputs
        predict = jnp.dot(trans_step, state, precision=lax.Precision.HIGHEST)
        state = keep_step * predict + drive_step
        return (state, (state, predict))

    last_state, (filtered, predicted) = lax.scan(
        update, start_state, (dense_steps, keep_rows, drive_terms)
    )
    return (last_state, filtered, predicted)


def run_smoother(dense_steps, filtered, predicted, smooth_gain, carried_in):

    def update(carried, inputs):
        trans_step, state, predict = inputs
        smooth_now = state + smooth_gain * carried
        residual = smooth_now - predict
        carried = jnp.dot(residual, trans_step, precision=lax.Precision.HIGHEST)
        return (carried, (smooth_now, residual))

    first_carry, (smoothed, residuals) = lax.scan(
        update, carried_in, (dense_steps, filtered, predicted), reverse=True
    )
    return (first_carry, smoothed, residuals)


def shards(transitions, pattern, obs_mask, measured, prior_mean, filter_gain, smooth_gain):
    highest = lax.Precision.HIGHEST
    dense_steps = masked_dense(transitions, pattern)
    state_width = dense_steps.shape[1]
    count_steps = dense_steps.shape[0]
    mask_rows = obs_mask[0].astype(jnp.float32)
    keep_rows = 1.0 - filter_gain[None, :] * mask_rows
    drive_terms = filter_gain[None, :] * mask_rows * measured[0]
    filter_map = chain_product(keep_rows[:, :, None] * dense_steps)
    smoother_map = chain_product(smooth_gain[None, :, None] * dense_steps).T
    zero_vector = jnp.zeros((state_width,), jnp.float32)
    filter_shift, _, _ = run_filter(dense_steps, keep_rows, drive_terms, zero_vector)
    prior_state = prior_mean[0]
    identity = jnp.eye(state_width, dtype=jnp.float32)
    prefix_maps = entering(
        (filter_map, filter_shift), "tm", compose, (identity, zero_vector), False
    )
    start_state = jnp.dot(prefix_maps[0], prior_state, precision=highest) + prefix_maps[1]
    _, filtered, predicted = run_filter(dense_steps, keep_rows, drive_terms, start_state)
    smoother_shift, _, _ = run_smoother(dense_steps, filtered, predicted, smooth_gain, zero_vector)
    suffix_maps = entering(
        (smoother_map, smoother_shift), "tm", compose, (identity, zero_vector), True
    )
    carried_in = suffix_maps[1]
    _, smoothed, residuals = run_smoother(dense_steps, filtered, predicted, smooth_gain, carried_in)
    local_info = jnp.dot(residuals.T, residuals, precision=highest)
    total_info = lax.psum(local_info, ("tm", "exp"))
    information = total_info / (count_steps * lax.axis_size("tm") * lax.axis_size("exp"))
    return (smoothed[None], information)


def solution(mesh):
    in_specs = (
        P("tm", None, None),
        P("tm", None, None),
        P("exp", "tm", None),
        P("exp", "tm", None),
        P("exp", None),
        P(),
        P(),
    )
    out_specs = (P("exp", "tm", None), P())
    return jax.shard_map(shards, mesh=mesh, in_specs=in_specs, out_specs=out_specs, check_vma=False)
```

profile of v0, /device:TPU:0, one launch (start us, length us, event | category | flops | bytes accessed | tf_op | source)
XLA Modules:
  0.0 665.8 jit_solution(17805602499832563561)
XLA Ops:
  8.1 11.2 %mul.71 = f32[64,4,64,4,64]{4,3,2,1,0:T(4,128)} broadcast(f32[64,4,4]{2,1,0:T(4,128)S(1)} %copy.10), dimensions={0,1,3} | broadcast | bytes 16781312 | tf_op jit(solution)/shard_map/mul | solution.py:29
  19.3 30.5 %mul.72 = f32[64,256,256]{2,1,0:T(8,128)} reshape(f32[64,4,64,4,64]{4,3,2,1,0:T(4,128)} %mul.71) | data formatting | bytes 33554432 | tf_op jit(solution)/shard_map/mul | solution.py:29
  49.8 17.7 %broadcast_multiply_fusion = (f32[64,256,256]{2,1,0:T(8,128)S(1)}, f32[64,256,256]{2,1,0:T(8,128)}) fusion(f32[64,256]{1,0:T(8,128)S(1)} %get-tuple-element.1043, f32[64,256,256]{2,1,0:T(8,128)} %param.19, f32[64,256,256]{2,1,0:T(8,128)} %mul.72), kind=kLoop, calls=%fused_computation.50 | loop fusion | flops 8388608 | bytes 67174400 | tf_op jit(solution)/shard_map/mul | solution.py:89
  67.6 10.7 %fusion.27 = f32[32,256,256]{2,1,0:T(8,128)} fusion(f32[64,256,256]{2,1,0:T(8,128)S(1)} %get-tuple-element.734), kind=kOutput, calls=%fused_computation.47 | convolution fusion | flops 6442450944 | bytes 25165824 | tf_op jit(solution)/shard_map/bij,bjk->bik/dot_general | solution.py:37
  78.2 8.4 %fusion.33 = f32[16,256,256]{2,1,0:T(8,128)S(1)} fusion(f32[32,256,256]{2,1,0:T(8,128)} %fusion.27), kind=kOutput, calls=%fused_computation.55 | convolution fusion | flops 3221225472 | bytes 12582912 | tf_op jit(solution)/shard_map/bij,bjk->bik/dot_general | solution.py:37
  86.7 2.2 fusion.39
  91.9 7.3 %broadcast_multiply_fusion.1 = f32[64,256,256]{2,1,0:T(8,128)S(1)} fusion(f32[64,256,256]{2,1,0:T(8,128)} %get-tuple-element.1124, f32[256]{0:T(256)S(1)} %copy-done.1), kind=kLoop, calls=%fused_computation.54 | loop fusion | flops 4194304 | bytes 33555456 | tf_op jit(solution)/shard_map/mul | solution.py:90
  99.1 10.7 %fusion.30 = f32[32,256,256]{2,1,0:T(8,128)} fusion(f32[64,256,256]{2,1,0:T(8,128)S(1)} %broadcast_multiply_fusion.1), kind=kOutput, calls=%fused_computation.51 | convolution fusion | flops 6442450944 | bytes 25165824 | tf_op jit(solution)/shard_map/bij,bjk->bik/dot_general | solution.py:37
  109.8 8.5 %fusion.36 = f32[16,256,256]{2,1,0:T(8,128)S(1)} fusion(f32[32,256,256]{2,1,0:T(8,128)} %fusion.30), kind=kOutput, calls=%fused_computation.58 | convolution fusion | flops 3221225472 | bytes 12582912 | tf_op jit(solution)/shard_map/bij,bjk->bik/dot_general | solution.py:37
  118.3 2.2 fusion.42
  123.8 85.5 %while.92 = (s32[]{:T(128)}, f32[256]{0:T(256)S(1)}, f32[64,256]{1,0:T(8,128)S(1)}, f32[64,256,256]{2,1,0:T(8,128)}, f32[64,256]{1,0:T(8,128)S(1)}, /*index=5*/s32[]{:T(128)}, s32[]{:T(128)}) while((s32[]{:T(128)}, f32[256]{0:T(256)S(1)}, f32[64,256]{1,0:T(8,128)S(1)}, f32[64,256,256]{2,1,0:T(8,128)}, f32[64,256]{1,0:T(8,128)S(1)}, ...), condition=%wide.region_1.2_spmd.clone, body=%wide.region_0.1_spmd.clone.sunk | while | flops 787203 | bytes 275035 | solution.py:60
  209.2 22.2 %all-gather.4 = f32[8,1,256]{2,1,0:T(1,128)S(1)} all-gather(f32[1,1,256]{2,1,0:T(1,128)S(1)} %bitcast.198), channel_id=4, replica_groups=mesh['tm'=8,'exp'=4] {'tm'}, dimensions={0}, use_global_device_ids=true | all-gather | bytes 9216 | tf_op jit(solution)/shard_map/all_gather | solution.py:9
  231.5 21.6 %while.93 = (s32[]{:T(128)}, f32[256,256]{1,0:T(8,128)S(1)}, f32[256]{0:T(256)S(1)}, s32[]{:T(128)}, f32[8,256,256]{2,1,0:T(8,128)}, /*index=5*/f32[8,256]{1,0:T(8,128)S(1)}, s32[]{:T(128)}, s32[]{:T(128)}) while((s32[]{:T(128)}, f32[256,256]{1,0:T(8,128)S(1)}, f32[256]{0:T(256)S(1)}, s32[]{:T(128)}, f32[8,256,256]{2,1,0:T(8,128)}, ...), condition=%wide.region_3.4_spmd.clone, body=%wide.region_2.3_spmd.clone.sunk | while | flops 202179584 | bytes 1846383 | solution.py:20
  238.2 1.3 convolution_select_fusion.2
  246.3 1.3 convolution_select_fusion.2
  249.0 1.3 convolution_select_fusion.2
  251.7 1.3 convolution_select_fusion.2
  253.5 90.9 %while.89 = (s32[]{:T(128)}, f32[256]{0:T(256)S(1)}, f32[64,256]{1,0:T(8,128)S(1)}, f32[64,256]{1,0:T(8,128)S(1)}, f32[64,256]{1,0:T(8,128)S(1)}, /*index=5*/f32...) while((s32[]{:T(128)}, f32[256]{0:T(256)S(1)}, f32[64,256]{1,0:T(8,128)S(1)}, ...), condition=%wide.region_5.6_spmd, body=%wide.region_4.5_spmd.sunk | while | flops 786946 | bytes 277097 | solution.py:60
  344.4 77.4 %while.90 = (s32[]{:T(128)}, f32[256]{0:T(256)S(1)}, f32[64,256]{1,0:T(8,128)S(1)}, f32[256]{0:T(256)S(1)}, f32[64,256]{1,0:T(8,128)S(1)}, /*index=5*/f32[64,256,256]{2,1,0:T(8,128)}, s32[]{:T(128)}, s32[]{:T(128)}) while((s32[]{:T(128)}, f32[256]{0:T(256)S(1)}, f32[64,256]{1,0:T(8,128)S(1)}, f32[256]{0:T(256)S(1)}, f32[64,256]{1,0:T(8,128)S(1)}, ...), condition=%wide.region_7.8_spmd, body=%wide.region_6.7_spmd.sunk | while | flops 787203 | bytes 273513 | solution.py:75
  421.8 16.3 %all-gather.5 = f32[8,1,256]{2,1,0:T(1,128)S(1)} all-gather(f32[1,1,256]{2,1,0:T(1,128)S(1)} %bitcast.197), channel_id=5, replica_groups=mesh['tm'=8,'exp'=4] {'tm'}, dimensions={0}, use_global_device_ids=true | all-gather | bytes 9216 | tf_op jit(solution)/shard_map/all_gather | solution.py:9
  438.1 10.8 %while.94 = (s32[]{:T(128)}, f32[256]{0:T(256)S(1)}, s32[]{:T(128)}, f32[8,256,256]{2,1,0:T(8,128)}, f32[8,256]{1,0:T(8,128)S(1)}, /*index=5*/s32[]{:T(128)}, s32[]{:T(128)}, s32[]{:T(128)}, s32[]{:T(128)}) while((s32[]{:T(128)}, f32[256]{0:T(256)S(1)}, s32[]{:T(128)}, f32[8,256,256]{2,1,0:T(8,128)}, f32[8,256]{1,0:T(8,128)S(1)}, ...), condition=%wide.region_9.10_spmd.clone, body=%wide.region_8.9_spmd.clone.sunk | while | flops 787464 | bytes 272552 | solution.py:20
  448.9 83.7 %while.91 = (s32[]{:T(128)}, f32[256]{0:T(256)S(1)}, f32[64,256]{1,0:T(8,128)S(1)}, f32[64,256]{1,0:T(8,128)S(1)}, f32[64,256]{1,0:T(8,128)S(1)}, /*index=5*/f32...) while((s32[]{:T(128)}, f32[256]{0:T(256)S(1)}, ...), condition=%wide.region_11.12_spmd, body=%wide.region_10.11_spmd.sunk | while | flops 787203 | bytes 278665 | solution.py:75
  533.7 123.9 %all-reduce.2.cloned.1.call-done = f32[256,256]{1,0:T(8,128)} async-done(((f32[256,256]{1,0:T(8,128)}), f32[256,256]{1,0:T(8,128)}) %all-reduce.2.cloned.1.call-update) | async-done | bytes 262160 | tf_op jit(solution)/shard_map/psum | solution.py:107
  657.6 1.7 broadcast_multiply_fusion.2
  (1207 shorter events, 363.2 us)
Async XLA Ops:
  7.2 245.9 %copy-start = (f32[1,256]{1,0:T(1,128)S(1)}, f32[1,256]{1,0:T(1,128)}, u32[]{:S(2)}) copy-start(f32[1,256]{1,0:T(1,128)} %param.23) | copy-start | bytes 3076
  7.2 224.3 %all-gather.11.cloned.1.call-start = ((), (), s32[]{:S(2)}) async-start(), calls=%async_computation.2 | async-start | bytes 2359296 | tf_op jit(solution)/shard_map/all_gather | solution.py:9
  19.3 30.5 %copy-start.3 = (f32[1,64,256]{2,1,0:T(8,128)S(1)}, f32[1,64,256]{2,1,0:T(8,128)}, u32[]{:S(2)}) copy-start(f32[1,64,256]{2,1,0:T(8,128)} %param.22) | copy-start | bytes 196612
  19.3 30.5 %copy-start.4 = (s32[1,64,256]{2,1,0:T(8,128)S(1)}, s32[1,64,256]{2,1,0:T(8,128)}, u32[]{:S(2)}) copy-start(s32[1,64,256]{2,1,0:T(8,128)} %param.21) | copy-start | bytes 196612
  19.3 30.5 %copy-start.5 = (f32[256]{0:T(256)S(1)}, f32[256]{0:T(256)}, u32[]{:S(2)}) copy-start(f32[256]{0:T(256)} %param.24) | copy-start | bytes 3076
  86.6 5.2 copy-start.1
  91.8 346.3 %all-gather.9.cloned.1.call-start = ((), (), s32[]{:S(2)}) async-start(), calls=%async_computation.1 | async-start | bytes 2359296 | tf_op jit(solution)/shard_map/all_gather | solution.py:9
  123.6 534.0 %all-reduce.2.cloned.1.call-start = ((), (), s32[]{:S(2)}) async-start(), calls=%async_computation | async-start | bytes 524288 | tf_op jit(solution)/shard_map/psum | solution.py:107
  532.6 126.7 %copy-start.2 = (f32[64,256]{1,0:T(8,128)}, f32[64,256]{1,0:T(8,128)S(1)}, u32[]{:S(2)}) copy-start(f32[64,256]{1,0:T(8,128)S(1)} %get-tuple-element.599) | copy-start | bytes 196612
Sparse Core Ops, SparseCore 0:
  91.9 52.1 all-gather.10
  146.8 47.8 all-gather.8
  533.9 123.7 all-reduce.1
where the time goes:
time: 676 us; the launch traced here: 666 us
  matrix products  383 us (57%)
  waiting for transfers between devices  124 us (18%)
  local copies, waits for them, and re-layouts  63 us (9%)
  blocking collectives  38.6 us (6%)
  other arithmetic  33 us (5%)
  between operations  14 us (2%)
  loops' own time  9.82 us (1%)
    dot_general x128, matrix products, update(): predict = jnp.dot(trans_step, state, precision=lax.Precision.HIGHEST)  157 us
    dot_general x128, matrix products, update(): carried = jnp.dot(residual, trans_step, precision=lax.Precision.HIGHEST)  146 us
    psum x1, waiting for transfers between devices, shards(): total_info = lax.psum(local_info, ('tm', 'exp'))  124 us
    dot_general x12, matrix products, chain_product(): jnp.einsum('bij,bjk->bik', later_maps, earlier_maps, precision=lax.Precis...  48.6 us
    mul x2, local copies, waits for them, and re-layouts, masked_dense(): return (reshaped * weights).reshape(count_steps, state_width, state_width)  41.7 us
    all_gather x2, blocking collectives, entering(): everything = jax.tree.map(lambda part: lax.all_gather(part, axis), x)  38.6 us
    dot_general x16, matrix products, compose(): jnp.dot(later_maps[0], earlier_maps[1], precision=highest) + later_maps[1]  19.6 us
    mul x1, other arithmetic, shards(): filter_map = chain_product(keep_rows[:, :, None] * dense_steps)  17.7 us
  transfers between devices with their start and end apart: 3, of which 1 were waited for; matrix products, arithmetic and copies ran while one was open for 45% of the time, Pallas kernels for 0%

commit v1 on v0

--- a/solution.py
+++ b/solution.py
@@ -104,7 +104,7 @@
     carried_in = suffix_maps[1]
     _, smoothed, residuals = run_smoother(dense_steps, filtered, predicted, smooth_gain, carried_in)
     local_info = jnp.dot(residuals.T, residuals, precision=highest)
-    total_info = lax.psum(local_info, ("tm", "exp"))
+    total_info = jnp.sum(lax.all_gather(local_info, ("tm", "exp")), axis=0)
     information = total_info / (count_steps * lax.axis_size("tm") * lax.axis_size("exp"))
     return (smoothed[None], information)
 

time: 676 us -> 631 us (0.933)
  waiting for transfers between devices: 124 us -> 76.5 us
    psum x1 -> x0, waiting for transfers between devices: 124 us -> none  [shards(): total_info = lax.psum(local_info, ('tm', 'exp'))]
    all_gather x0 -> x1, waiting for transfers between devices: none -> 76.5 us  [shards(): total_info = jnp.sum(lax.all_gather(local_info, ('tm', 'exp')), axis=0)]
  transfers between devices with their start and end apart: 3 -> 3, of which waited for: 1 -> 1; matrix products, arithmetic and copies ran while one was open for 45% -> 48% of each run, Pallas kernels for 0% -> 0%
where the time goes in v1:
time: 631 us; the launch traced here: 621 us
  matrix products  383 us (61%)
  waiting for transfers between devices  76.5 us (12%)
  local copies, waits for them, and re-layouts  63 us (10%)
  blocking collectives  38.6 us (6%)
  other arithmetic  36 us (6%)
  between operations  14 us (2%)
  loops' own time  9.82 us (2%)
    dot_general x128, matrix products, update(): predict = jnp.dot(trans_step, state, precision=lax.Precision.HIGHEST)  157 us
    dot_general x128, matrix products, update(): carried = jnp.dot(residual, trans_step, precision=lax.Precision.HIGHEST)  146 us
    all_gather x1, waiting for transfers between devices, shards(): total_info = jnp.sum(lax.all_gather(local_info, ('tm', 'exp')), axis=0)  76.5 us
    dot_general x12, matrix products, chain_product(): jnp.einsum('bij,bjk->bik', later_maps, earlier_maps, precision=lax.Precis...  48.6 us
    mul x2, local copies, waits for them, and re-layouts, masked_dense(): return (reshaped * weights).reshape(count_steps, state_width, state_width)  41.7 us
    all_gather x2, blocking collectives, entering(): everything = jax.tree.map(lambda part: lax.all_gather(part, axis), x)  38.6 us
    dot_general x16, matrix products, compose(): jnp.dot(later_maps[0], earlier_maps[1], precision=highest) + later_maps[1]  19.6 us
    mul x1, other arithmetic, shards(): filter_map = chain_product(keep_rows[:, :, None] * dense_steps)  17.7 us
  transfers between devices with their start and end apart: 3, of which 1 were waited for; matrix products, arithmetic and copies ran while one was open for 48% of the time, Pallas kernels for 0%

profile of v1, /device:TPU:0, one launch (start us, length us, event | category | flops | bytes accessed | tf_op | source)
XLA Modules:
  0.0 621.4 jit_solution(11062786701597148592)
XLA Ops:
  8.1 11.2 %mul.71 = f32[64,4,64,4,64]{4,3,2,1,0:T(4,128)} broadcast(f32[64,4,4]{2,1,0:T(4,128)S(1)} %copy.10), dimensions={0,1,3} | broadcast | bytes 16781312 | tf_op jit(solution)/shard_map/mul | solution.py:29
  19.3 30.5 %mul.72 = f32[64,256,256]{2,1,0:T(8,128)} reshape(f32[64,4,64,4,64]{4,3,2,1,0:T(4,128)} %mul.71) | data formatting | bytes 33554432 | tf_op jit(solution)/shard_map/mul | solution.py:29
  49.8 17.7 %broadcast_multiply_fusion = (f32[64,256,256]{2,1,0:T(8,128)S(1)}, f32[64,256,256]{2,1,0:T(8,128)}) fusion(f32[64,256]{1,0:T(8,128)S(1)} %get-tuple-element.1043, f32[64,256,256]{2,1,0:T(8,128)} %param.19, f32[64,256,256]{2,1,0:T(8,128)} %mul.72), kind=kLoop, calls=%fused_computation.50 | loop fusion | flops 8388608 | bytes 67174400 | tf_op jit(solution)/shard_map/mul | solution.py:89
  67.6 10.7 %fusion.27 = f32[32,256,256]{2,1,0:T(8,128)} fusion(f32[64,256,256]{2,1,0:T(8,128)S(1)} %get-tuple-element.734), kind=kOutput, calls=%fused_computation.47 | convolution fusion | flops 6442450944 | bytes 25165824 | tf_op jit(solution)/shard_map/bij,bjk->bik/dot_general | solution.py:37
  78.2 8.4 %fusion.33 = f32[16,256,256]{2,1,0:T(8,128)S(1)} fusion(f32[32,256,256]{2,1,0:T(8,128)} %fusion.27), kind=kOutput, calls=%fused_computation.55 | convolution fusion | flops 3221225472 | bytes 12582912 | tf_op jit(solution)/shard_map/bij,bjk->bik/dot_general | solution.py:37
  86.7 2.2 fusion.39
  91.9 7.3 %broadcast_multiply_fusion.1 = f32[64,256,256]{2,1,0:T(8,128)S(1)} fusion(f32[64,256,256]{2,1,0:T(8,128)} %get-tuple-element.1124, f32[256]{0:T(256)S(1)} %copy-done.1), kind=kLoop, calls=%fused_computation.54 | loop fusion | flops 4194304 | bytes 33555456 | tf_op jit(solution)/shard_map/mul | solution.py:90
  99.1 10.7 %fusion.30 = f32[32,256,256]{2,1,0:T(8,128)} fusion(f32[64,256,256]{2,1,0:T(8,128)S(1)} %broadcast_multiply_fusion.1), kind=kOutput, calls=%fused_computation.51 | convolution fusion | flops 6442450944 | bytes 25165824 | tf_op jit(solution)/shard_map/bij,bjk->bik/dot_general | solution.py:37
  109.8 8.5 %fusion.36 = f32[16,256,256]{2,1,0:T(8,128)S(1)} fusion(f32[32,256,256]{2,1,0:T(8,128)} %fusion.30), kind=kOutput, calls=%fused_computation.58 | convolution fusion | flops 3221225472 | bytes 12582912 | tf_op jit(solution)/shard_map/bij,bjk->bik/dot_general | solution.py:37
  118.3 2.2 fusion.42
  123.8 85.5 %while.92 = (s32[]{:T(128)}, f32[256]{0:T(256)S(1)}, f32[64,256]{1,0:T(8,128)S(1)}, f32[64,256,256]{2,1,0:T(8,128)}, f32[64,256]{1,0:T(8,128)S(1)}, /*index=5*/s32[]{:T(128)}, s32[]{:T(128)}) while((s32[]{:T(128)}, f32[256]{0:T(256)S(1)}, f32[64,256]{1,0:T(8,128)S(1)}, f32[64,256,256]{2,1,0:T(8,128)}, f32[64,256]{1,0:T(8,128)S(1)}, ...), condition=%wide.region_1.2_spmd.clone, body=%wide.region_0.1_spmd.clone.sunk | while | flops 787203 | bytes 275035 | solution.py:60
  209.2 22.2 %all-gather.5 = f32[8,1,256]{2,1,0:T(1,128)S(1)} all-gather(f32[1,1,256]{2,1,0:T(1,128)S(1)} %bitcast.200), channel_id=4, replica_groups=mesh['tm'=8,'exp'=4] {'tm'}, dimensions={0}, use_global_device_ids=true | all-gather | bytes 9216 | tf_op jit(solution)/shard_map/all_gather | solution.py:9
  231.5 21.6 %while.93 = (s32[]{:T(128)}, f32[256,256]{1,0:T(8,128)S(1)}, f32[256]{0:T(256)S(1)}, s32[]{:T(128)}, f32[8,256,256]{2,1,0:T(8,128)}, /*index=5*/f32[8,256]{1,0:T(8,128)S(1)}, s32[]{:T(128)}, s32[]{:T(128)}) while((s32[]{:T(128)}, f32[256,256]{1,0:T(8,128)S(1)}, f32[256]{0:T(256)S(1)}, s32[]{:T(128)}, f32[8,256,256]{2,1,0:T(8,128)}, ...), condition=%wide.region_3.4_spmd.clone, body=%wide.region_2.3_spmd.clone.sunk | while | flops 202179584 | bytes 1846383 | solution.py:20
  238.2 1.3 convolution_select_fusion.2
  246.3 1.3 convolution_select_fusion.2
  249.0 1.3 convolution_select_fusion.2
  251.7 1.3 convolution_select_fusion.2
  253.5 90.9 %while.89 = (s32[]{:T(128)}, f32[256]{0:T(256)S(1)}, f32[64,256]{1,0:T(8,128)S(1)}, f32[64,256]{1,0:T(8,128)S(1)}, f32[64,256]{1,0:T(8,128)S(1)}, /*index=5*/f32...) while((s32[]{:T(128)}, f32[256]{0:T(256)S(1)}, f32[64,256]{1,0:T(8,128)S(1)}, ...), condition=%wide.region_5.6_spmd, body=%wide.region_4.5_spmd.sunk | while | flops 786946 | bytes 277097 | solution.py:60
  344.4 77.4 %while.90 = (s32[]{:T(128)}, f32[256]{0:T(256)S(1)}, f32[64,256]{1,0:T(8,128)S(1)}, f32[256]{0:T(256)S(1)}, f32[64,256]{1,0:T(8,128)S(1)}, /*index=5*/f32[64,256,256]{2,1,0:T(8,128)}, s32[]{:T(128)}, s32[]{:T(128)}) while((s32[]{:T(128)}, f32[256]{0:T(256)S(1)}, f32[64,256]{1,0:T(8,128)S(1)}, f32[256]{0:T(256)S(1)}, f32[64,256]{1,0:T(8,128)S(1)}, ...), condition=%wide.region_7.8_spmd, body=%wide.region_6.7_spmd.sunk | while | flops 787203 | bytes 273513 | solution.py:75
  421.8 16.3 %all-gather.6 = f32[8,1,256]{2,1,0:T(1,128)S(1)} all-gather(f32[1,1,256]{2,1,0:T(1,128)S(1)} %bitcast.199), channel_id=5, replica_groups=mesh['tm'=8,'exp'=4] {'tm'}, dimensions={0}, use_global_device_ids=true | all-gather | bytes 9216 | tf_op jit(solution)/shard_map/all_gather | solution.py:9
  438.1 10.8 %while.94 = (s32[]{:T(128)}, f32[256]{0:T(256)S(1)}, s32[]{:T(128)}, f32[8,256,256]{2,1,0:T(8,128)}, f32[8,256]{1,0:T(8,128)S(1)}, /*index=5*/s32[]{:T(128)}, s32[]{:T(128)}, s32[]{:T(128)}, s32[]{:T(128)}) while((s32[]{:T(128)}, f32[256]{0:T(256)S(1)}, s32[]{:T(128)}, f32[8,256,256]{2,1,0:T(8,128)}, f32[8,256]{1,0:T(8,128)S(1)}, ...), condition=%wide.region_9.10_spmd.clone, body=%wide.region_8.9_spmd.clone.sunk | while | flops 787464 | bytes 272552 | solution.py:20
  448.9 83.7 %while.91 = (s32[]{:T(128)}, f32[256]{0:T(256)S(1)}, f32[64,256]{1,0:T(8,128)S(1)}, f32[64,256]{1,0:T(8,128)S(1)}, f32[64,256]{1,0:T(8,128)S(1)}, /*index=5*/f32...) while((s32[]{:T(128)}, f32[256]{0:T(256)S(1)}, ...), condition=%wide.region_11.12_spmd, body=%wide.region_10.11_spmd.sunk | while | flops 787203 | bytes 278665 | solution.py:75
  533.7 76.5 %all-gather.15.cloned.1.call-done = f32[8192,256]{1,0:T(8,128)} async-done(((f32[256,256]{1,0:T(8,128)}), f32[8192,256]{1,0:T(8,128)}) %all-gather.15.cloned.1.call-update) | async-done | bytes 8388624 | tf_op jit(solution)/shard_map/all_gather | solution.py:107
  610.2 3.9 reduce_sum.9
  (1208 shorter events, 364.0 us)
Async XLA Ops:
  7.2 245.9 %copy-start = (f32[1,256]{1,0:T(1,128)S(1)}, f32[1,256]{1,0:T(1,128)}, u32[]{:S(2)}) copy-start(f32[1,256]{1,0:T(1,128)} %param.23) | copy-start | bytes 3076
  7.2 224.3 %all-gather.13.cloned.1.call-start = ((), (), s32[]{:S(2)}) async-start(), calls=%async_computation.1 | async-start | bytes 2359296 | tf_op jit(solution)/shard_map/all_gather | solution.py:9
  19.3 30.5 %copy-start.3 = (f32[1,64,256]{2,1,0:T(8,128)S(1)}, f32[1,64,256]{2,1,0:T(8,128)}, u32[]{:S(2)}) copy-start(f32[1,64,256]{2,1,0:T(8,128)} %param.22) | copy-start | bytes 196612
  19.3 30.5 %copy-start.4 = (s32[1,64,256]{2,1,0:T(8,128)S(1)}, s32[1,64,256]{2,1,0:T(8,128)}, u32[]{:S(2)}) copy-start(s32[1,64,256]{2,1,0:T(8,128)} %param.21) | copy-start | bytes 196612
  19.3 30.5 %copy-start.5 = (f32[256]{0:T(256)S(1)}, f32[256]{0:T(256)}, u32[]{:S(2)}) copy-start(f32[256]{0:T(256)} %param.24) | copy-start | bytes 3076
  86.6 5.2 copy-start.1
  91.8 346.3 %all-gather.11.cloned.1.call-start = ((), (), s32[]{:S(2)}) async-start(), calls=%async_computation | async-start | bytes 2359296 | tf_op jit(solution)/shard_map/all_gather | solution.py:9
  123.6 486.5 %all-gather.15.cloned.1.call-start = ((), (), s32[]{:S(2)}) async-start(), calls=%async_computation.2 | async-start | bytes 8650752 | tf_op jit(solution)/shard_map/all_gather | solution.py:107
  532.6 82.3 %copy-start.2 = (f32[64,256]{1,0:T(8,128)}, f32[64,256]{1,0:T(8,128)S(1)}, u32[]{:S(2)}) copy-start(f32[64,256]{1,0:T(8,128)S(1)} %get-tuple-element.599) | copy-start | bytes 196612
Sparse Core Ops, SparseCore 0:
  91.9 52.1 all-gather.12
  146.8 47.8 all-gather.10
  533.9 76.2 all-gather.14
